TPU v7x, 32 devices: a whole 2x2x4 slice. The times are simulated.
32 devices in a mesh: grp: 2 (over x), row: 8 (over z, y), col: 2 (over core).
Axes of the slice: x: 2, y: 2, z: 4, core: 2. Of those that a mesh axis runs over, the one named last changes fastest.
Arguments:
- pair_act: bfloat16 [64, 32, 128], P(('grp', 'row'), 'col'), parts along dimension 0, may hold values from -200 to 200
- cotangent: bfloat16 [64, 32, 128], P(('grp', 'row'), 'col'), parts along dimension 0, may hold values from -6 to 6
- residue_mask: int32 [64], P('grp'), parts along dimension 0, may hold values from 0 to 1, as said below
- front_weight: bfloat16 [2, 128, 640], replicated, may hold values from -0.5 to 0.5
- out_weight: bfloat16 [2, 128, 128], replicated, may hold values from -0.5 to 0.5
Outputs:
- pair_grad: bfloat16 [64, 32, 128], P(('grp', 'row'), 'col'), parts along dimension 0
There are 2 independent parts, one for each index of `grp`. A program takes and returns all parts, laid end to end along the dimension named above; an argument that names none is the same for every part. Nothing has to cross between parts.
Inputs may be any that keep to these rules, and one draw needn't show every extreme that they name: residue_mask is 1 on residues 0 to L - 1 and 0 from L on, for a chain length L of at least 24.
All inputs are finite; a program needn't handle non-finite values.
Results may differ from a plain program's by a relative error of at most 0.01.
Values may be sent and summed in bfloat16 or wider, within the bound.
No kernel may reach another device: no remote copies, remote signals or barrier semaphores. Data moves between devices by JAX's collectives and lax.ppermute only.
A program may use at most 64 MiB of HBM per device.

v0:
```python
import functools

import jax
import jax.numpy as jnp
from jax import lax
from jax.experimental import pallas as pl
from jax.experimental.pallas import tpu as pltpu
from jax.sharding import PartitionSpec as P

H = 128
EPS = 1e-05
PAD = 4
VMEM_BUDGET = 40 << 20
F32 = jnp.float32
BF16 = jnp.bfloat16


def from_root(array, axis, root):
    mine = lax.axis_index(axis) == root
    return lax.psum(jnp.where(mine, array, jnp.zeros_like(array)), axis)


def layer_norm(values):
    centred = values - jnp.mean(values, axis=-1, keepdims=True)
    spread = jnp.mean(centred * centred, axis=-1, keepdims=True)
    return centred * lax.rsqrt(spread + 1e-05)


def project_pair(inner_pair, mask_pair, weight):
    normed = layer_norm(inner_pair.astype(jnp.float32)).astype(jnp.bfloat16)
    linear = jnp.dot(normed, weight, preferred_element_type=jnp.float32)
    left_side = jax.nn.sigmoid(linear[..., :H]) * linear[..., H : 2 * H]
    right_side = jax.nn.sigmoid(linear[..., 2 * H : 3 * H]) * linear[..., 3 * H : 4 * H]
    operands = (jnp.stack((left_side, right_side)) * mask_pair[None, :, :, None]).astype(
        jnp.bfloat16
    )
    return (operands, jax.nn.sigmoid(linear[..., 4 * H :]))


def finish(mixed_part, gate_value, inner_pair, weight):
    normed = layer_norm(mixed_part).astype(jnp.bfloat16)
    update = jnp.dot(normed, weight, preferred_element_type=jnp.float32)
    return (inner_pair.astype(jnp.float32) + gate_value * update).astype(jnp.bfloat16)


def spread_body(pair_act, cotangent, residue_mask, front_weight, out_weight):
    local_rows = pair_act.shape[0]
    local_cols = pair_act.shape[1]
    row_index = lax.axis_index("row")
    col_index = lax.axis_index("col")
    block_rows = lax.axis_size("row") // lax.axis_size("col")
    owner_col = row_index // block_rows
    offset = row_index % block_rows * local_rows
    chain_mask = residue_mask.astype(jnp.float32)
    mask_rows = lax.dynamic_slice_in_dim(chain_mask, row_index * local_rows, local_rows)
    mask_cols = lax.dynamic_slice_in_dim(chain_mask, col_index * local_cols, local_cols)
    mask_pair = mask_rows[:, None] * mask_cols[None, :]

    def gather_rows(stacked):
        return lax.all_gather(stacked, "row", axis=1, tiled=True)

    def column_block(gathered):
        slab = lax.dynamic_slice_in_dim(gathered, offset, local_rows, 1)
        return from_root(slab, "col", owner_col)

    def gather_cols(values):
        return lax.all_gather(values, "col", axis=1, tiled=True)

    def sum_cols(partial_term):
        return lax.psum_scatter(
            partial_term.astype(jnp.bfloat16), "col", scatter_dimension=1, tiled=True
        ).astype(jnp.float32)

    (out_ops, out_gate), out_front_back = jax.vjp(
        lambda inner_pair: project_pair(inner_pair, mask_pair, front_weight[0]), pair_act
    )
    fetched = gather_rows(out_ops)
    out_mixed = sum_cols(
        jnp.einsum("ikc,jkc->ijc", out_ops[0], fetched[-1], preferred_element_type=jnp.float32)
    )
    pair_mid, out_finish_back = jax.vjp(
        lambda mixed_part, gate_value, inner_pair: finish(
            mixed_part, gate_value, inner_pair, out_weight[0]
        ),
        out_mixed,
        out_gate,
        pair_act,
    )
    (in_ops, in_gate), in_front_back = jax.vjp(
        lambda inner_pair: project_pair(inner_pair, mask_pair, front_weight[1]), pair_mid
    )
    in_fetched = gather_rows(in_ops)
    left_block = column_block(in_fetched[0])
    in_mixed = jnp.einsum(
        "kic,kjc->ijc", left_block, in_fetched[1], preferred_element_type=jnp.float32
    )
    _, in_finish_back = jax.vjp(
        lambda mixed_part, gate_value, inner_pair: finish(
            mixed_part, gate_value, inner_pair, out_weight[1]
        ),
        in_mixed,
        in_gate,
        pair_mid,
    )
    grad_mixed, grad_gate, grad_inner = in_finish_back(cotangent)
    signal = grad_mixed.astype(jnp.bfloat16)
    signal_rows = gather_rows(signal[None])[0]
    left_rows = gather_cols(in_ops[0])
    grad_right = jnp.einsum(
        "kic,ijc->kjc", left_rows, signal_rows, preferred_element_type=jnp.float32
    )
    grad_left = sum_cols(
        jnp.einsum("kjc,ijc->kic", in_ops[1], signal_rows, preferred_element_type=jnp.float32)
    )
    (grad_front,) = in_front_back(
        (jnp.stack((grad_left, grad_right)).astype(jnp.bfloat16), grad_gate)
    )
    grad_mid = (grad_inner.astype(jnp.float32) + grad_front.astype(jnp.float32)).astype(
        jnp.bfloat16
    )
    grad_mixed, grad_gate, grad_inner = out_finish_back(grad_mid)
    signal = grad_mixed.astype(jnp.bfloat16)
    signal_cols = gather_cols(signal)
    grad_left = jnp.einsum(
        "ijc,jkc->ikc", signal_cols, fetched[-1], preferred_element_type=jnp.float32
    )
    signal_block = column_block(gather_rows(signal[None])[0])
    grad_right = jnp.einsum(
        "ijc,ikc->jkc", signal_block, fetched[0], preferred_element_type=jnp.float32
    )
    (grad_front,) = out_front_back(
        (jnp.stack((grad_left, grad_right)).astype(jnp.bfloat16), grad_gate)
    )
    return (grad_inner.astype(jnp.float32) + grad_front.astype(jnp.float32)).astype(jnp.bfloat16)


def sigmoid(values):
    return 0.5 + 0.5 * jnp.tanh(0.5 * values)


def lane_mean(values):
    return jnp.mean(values, axis=-1, keepdims=True)


def normalize(values):
    centred = values - lane_mean(values)
    inverse = lax.rsqrt(lane_mean(centred * centred) + EPS)
    return centred * inverse, inverse


def normalize_back(grad, normed, inverse):
    return inverse * (grad - lane_mean(grad) - normed * lane_mean(grad * normed))


def rounded(values):
    return values.astype(BF16).astype(F32)


def matmul(values, weight):
    return jnp.dot(values.astype(BF16), weight, preferred_element_type=F32)


def matmul_t(values, weight):
    return lax.dot_general(
        values.astype(BF16), weight, (((1,), (1,)), ((), ())), preferred_element_type=F32
    )


def split(linear):
    return [linear[:, i * H : (i + 1) * H] for i in range(5)]


def front_back(linear, mask, grad_left, grad_right, grad_gate, weight, normed, inverse):
    gate_l, val_l, gate_r, val_r, gate = split(linear)
    gate_l, gate_r, gate = sigmoid(gate_l), sigmoid(gate_r), sigmoid(gate)
    grad_left, grad_right = grad_left * mask, grad_right * mask
    pieces = (
        grad_left * val_l * (gate_l * (1.0 - gate_l)),
        grad_left * gate_l,
        grad_right * val_r * (gate_r * (1.0 - gate_r)),
        grad_right * gate_r,
        grad_gate * (gate * (1.0 - gate)),
    )
    grad = jnp.concatenate([piece.astype(BF16) for piece in pieces], axis=1)
    return rounded(normalize_back(rounded(matmul_t(grad, weight)), normed, inverse))


def chain_length(mask_ref):
    return jnp.sum(mask_ref[...], axis=1, keepdims=True).astype(jnp.int32)


def pair_mask(chain, count, span, start, offset):
    major = lax.broadcasted_iota(jnp.int32, (count, span, H), 0) + start
    minor = lax.broadcasted_iota(jnp.int32, (count, span, H), 1) + offset
    inside = jnp.maximum(major, minor).reshape(count * span, H) < chain
    return jnp.where(inside, 1.0, 0.0)


def projection(weight, source, mask):
    normed, _ = normalize(source)
    gate_l, val_l, gate_r, val_r, gate = split(matmul(normed, weight))
    return (
        rounded(mask * (sigmoid(gate_l) * val_l)),
        rounded(mask * (sigmoid(gate_r) * val_r)),
        sigmoid(gate),
    )


def product(count, span, row_of, ref_a, ref_b, pitch, minor, width):
    totals = [None] * count
    for s in range(span):
        block = ref_b[pl.ds(s * pitch + minor, width), :]
        for p in range(count):
            term = jnp.broadcast_to(ref_a[pl.ds(row_of(p, s), 1), :], (width, H)) * block
            totals[p] = term if totals[p] is None else totals[p] + term
    return totals


def half_kernel(
    n, rows, cols, blocks, mask_ref, own_ref, weight_ref, left, right, gate, part, act, right_t,
):
    pitch = n + PAD
    row_index = lax.axis_index("row")
    chain = chain_length(mask_ref)
    for position, block in enumerate(blocks):
        place = (row_index ^ block) * rows
        for a in range(rows):
            where = pl.ds(pl.multiple_of((place + a) * cols, cols), cols)
            act[where, :] = own_ref[position, a].astype(F32)
    mask = pair_mask(chain, n, cols, 0, lax.axis_index("col") * cols)
    a, b, g = projection(weight_ref[0, :, : 5 * H], act[...], mask)
    left[...] = a
    right[...] = b
    gate[...] = g
    for i in range(n):
        right_t[pl.ds(i, cols, stride=pitch), :] = b[i * cols : (i + 1) * cols]
    for start in range(0, n, rows):
        totals = product(
            rows, cols, lambda p, s: (start + p) * cols + s, left, right_t, pitch, 0, n)
        part[pl.ds(start * n, rows * n), :] = jnp.concatenate(totals, axis=0)


def access(n, rows, cols, blocks, mask_ref):
    pitch = n + PAD
    row_index = lax.axis_index("row")
    col_index = lax.axis_index("col")
    chain = chain_length(mask_ref)
    me = row_index * rows
    mine = pl.multiple_of(col_index * cols, cols)
    theirs = pl.multiple_of((1 - col_index) * cols, cols)
    step = rows * n

    def mask_of(count, span, start, offset):
        return pair_mask(chain, count, span, start, offset)

    def get(ref, start=0, count=n):
        return jnp.concatenate(
            [ref[pl.ds((start + a) * pitch, n), :] for a in range(count)], axis=0
        )

    def put(ref, start, values, count=n):
        for a in range(count):
            ref[pl.ds((start + a) * pitch, n), :] = values[a * n : (a + 1) * n]

    def put_t(ref, values):
        for a in range(n):
            ref[pl.ds(a, n, stride=pitch), :] = values[a * n : (a + 1) * n]

    def get_t(ref):
        return [ref[pl.ds(me + a, n, stride=pitch), :] for a in range(rows)]

    def take(ref):
        return jnp.concatenate([get(ref, me, rows)] + get_t(ref), axis=0)

    def own(ref, base, stride):
        return jnp.concatenate(
            [ref[pl.ds(base + a * stride + mine, cols), :] for a in range(rows)], axis=0)

    def place(ref, own_ref, other_ref):
        for position, block in enumerate(blocks):
            start = (row_index ^ block) * rows
            for a in range(rows):
                base = (start + a) * pitch
                ref[pl.ds(base + mine, cols), :] = own_ref[position, a].astype(F32)
                ref[pl.ds(base + theirs, cols), :] = other_ref[position, a].astype(F32)

    return me, mine, theirs, step, pitch, mask_of, place, get, put, put_t, take, own


def outgoing_kernel(
    n, rows, cols, blocks, mask_ref, own_ref, other_ref, weight_ref,
    half_left, half_right, half_gate, part, act, left, right, gate0, mixed0, right_t,
):
    (_, mine, theirs, _, pitch, mask_of, place, _, put, _, _, _) = access(
        n, rows, cols, blocks, mask_ref)
    front_ref = weight_ref.at[:, :, : 5 * H]
    place(act, own_ref, other_ref)

    source = jnp.concatenate(
        [act[pl.ds(i * pitch + theirs, cols), :] for i in range(n)], axis=0)
    a, b, g = projection(front_ref[0], source, mask_of(n, cols, 0, theirs))
    for i in range(n):
        these = slice(i * cols, (i + 1) * cols)
        right_t[pl.ds(i, cols, stride=pitch), :] = b[these]
        for ref, done, new in (
            (left, half_left, a), (right, half_right, b), (gate0, half_gate, g)):
            ref[pl.ds(i * pitch + theirs, cols), :] = new[these]
            ref[pl.ds(i * pitch + mine, cols), :] = done[pl.ds(i * cols, cols), :]

    for start in range(0, n, rows):
        totals = product(
            rows, cols, lambda p, s: (start + p) * pitch + theirs + s, left, right_t, pitch, 0, n)
        rest = part[pl.ds(start * n, rows * n), :]
        put(mixed0, start, jnp.concatenate(totals, axis=0) + rest, rows)


def incoming_kernel(
    n, rows, cols, blocks, mask_ref, weight_ref, act, gate0, mixed0,
    mid, left1, right1, left1_t, right1_t, gate1, mixed1,
):
    (_, _, _, _, pitch, mask_of, _, get, put, put_t, _, _) = access(
        n, rows, cols, blocks, mask_ref)
    front_ref, out_ref = weight_ref.at[:, :, : 5 * H], weight_ref.at[:, :, 5 * H :]
    normed, _ = normalize(get(mixed0))
    value = rounded(get(act) + get(gate0) * matmul(normed, out_ref[0]))
    put(mid, 0, value)
    a, b, g = projection(front_ref[1], value, mask_of(n, n, 0, 0))
    put(left1, 0, a)
    put(right1, 0, b)
    put_t(left1_t, a)
    put_t(right1_t, b)
    put(gate1, 0, g)

    for start in range(0, n, rows):
        totals = product(rows, n, lambda p, s: s * pitch + start + p, left1, right1, pitch, 0, n)
        put(mixed1, start, jnp.concatenate(totals, axis=0), rows)


def backward_kernel(
    n, rows, cols, blocks, mask_ref, act_ref, own_ref, other_ref, weight_ref,
    left, right, gate0, mixed0, mid, left1, right1, left1_t, right1_t, gate1, mixed1,
    grad_ref, cot, sig, sig_t, grow, s_gate, s_sig, dl, dr,
):
    (me, mine, _, step, pitch, mask_of, place, get, put, put_t, take, own) = access(
        n, rows, cols, blocks, mask_ref)
    front_ref, out_ref = weight_ref.at[:, :, : 5 * H], weight_ref.at[:, :, 5 * H :]
    place(cot, own_ref, other_ref)

    normed, inverse = normalize(get(mixed1))
    grad = rounded(matmul_t(get(cot) * get(gate1), out_ref[1]))
    value = rounded(normalize_back(grad, normed, inverse))
    put(sig, 0, value)
    put_t(sig_t, value)

    def row_of(p, s):
        return (me + p) * pitch + s

    dl[pl.ds(0, step), :] = jnp.concatenate(
        product(rows, n, row_of, right1, sig_t, pitch, 0, n), axis=0)
    dl[pl.ds(step, step), :] = jnp.concatenate(
        product(rows, n, row_of, sig, right1_t, pitch, 0, n), axis=0)
    dr[pl.ds(0, step), :] = jnp.concatenate(
        product(rows, n, row_of, left1, sig, pitch, 0, n), axis=0)
    dr[pl.ds(step, step), :] = jnp.concatenate(
        product(rows, n, lambda p, s: s * pitch + me + p, sig, left1_t, pitch, 0, n), axis=0)

    mask_rows = mask_of(rows, n, me, 0)
    cot_s = take(cot)
    mixed, _ = normalize(take(mixed1))
    normed, inverse = normalize(take(mid))
    grad_gate = cot_s * matmul(mixed, out_ref[1])
    grad = front_back(
        matmul(normed, front_ref[1]), jnp.concatenate([mask_rows, mask_rows], axis=0),
        rounded(dl[...]), rounded(dr[...]), grad_gate, front_ref[1], normed, inverse)
    grad_mid = rounded(cot_s + grad)
    mixed, inverse = normalize(take(mixed0))
    grow[...] = grad_mid[:step]
    s_gate[...] = grad_mid[:step] * matmul(mixed[:step], out_ref[0])
    grad = rounded(matmul_t(grad_mid * take(gate0), out_ref[0]))
    s_sig[...] = rounded(normalize_back(grad, mixed, inverse))

    grad_left = product(rows, n, lambda p, s: p * n + s, s_sig, right, pitch, mine, cols)
    grad_right = product(rows, n, lambda p, s: step + p * n + s, s_sig, left, pitch, mine, cols)

    normed, inverse = normalize(act_ref[0].astype(F32).reshape(rows * cols, H))
    grad = front_back(
        matmul(normed, front_ref[0]), mask_of(rows, cols, me, mine),
        rounded(jnp.concatenate(grad_left, axis=0)), rounded(jnp.concatenate(grad_right, axis=0)),
        own(s_gate, 0, n), front_ref[0], normed, inverse)
    grad_ref[...] = (own(grow, 0, n) + grad).astype(BF16).reshape(rows, cols, H)


def whole_body(pair_act, cotangent, residue_mask, front_weight, out_weight):
    rows, cols, _ = pair_act.shape
    n = residue_mask.shape[0]
    row_count = lax.axis_size("row")
    bits = row_count.bit_length() - 1
    weights = jnp.concatenate((front_weight, out_weight), axis=2)
    mask = residue_mask.reshape(1, n).astype(F32)
    blocks = [0]
    steps = [1 << b for b in range(1, bits)] + [1]

    def swap(array, step):
        return lax.ppermute(array, "row", [(i, i ^ step) for i in range(row_count)])

    sent = (pair_act[None], cotangent[None])
    held = lax.optimization_barrier(jnp.stack(sent))
    held = (held[0], held[1])
    for step in steps:
        act_late = swap(sent[0], step)
        cot_late = swap(sent[1], step)
        act = jnp.concatenate((held[0], act_late))
        if step != steps[-1]:
            cot = jnp.concatenate((held[1], cot_late))
            sent = held = (act, cot)
        blocks = blocks + [b ^ step for b in blocks]
    act_other = lax.ppermute(act, "col", [(0, 1), (1, 0)])
    full = pltpu.VMEM((n * (n + PAD), H), F32)
    some = pltpu.VMEM((rows * n, H), F32)
    twice = pltpu.VMEM((2 * rows * n, H), F32)
    vmem = pl.BlockSpec(memory_space=pltpu.VMEM)
    part_of = jax.ShapeDtypeStruct((n * cols, H), F32)
    halves = pl.pallas_call(
        functools.partial(half_kernel, n, rows, cols, blocks),
        out_shape=[part_of] * 3 + [jax.ShapeDtypeStruct((n * n, H), F32)],
        in_specs=[vmem] * 3,
        out_specs=[vmem] * 4,
        scratch_shapes=[pltpu.VMEM((n * cols, H), F32), pltpu.VMEM((cols * (n + PAD), H), F32)],
        compiler_params=pltpu.CompilerParams(vmem_limit_bytes=VMEM_BUDGET // 4),
    )(mask, act, weights)
    pairs_of = jax.ShapeDtypeStruct((n * (n + PAD), H), F32)
    act_full, left, right, gate0, mixed0 = pl.pallas_call(
        functools.partial(outgoing_kernel, n, rows, cols, blocks),
        out_shape=[pairs_of] * 5,
        in_specs=[vmem] * 8,
        out_specs=[vmem] * 5,
        scratch_shapes=[full],
        compiler_params=pltpu.CompilerParams(vmem_limit_bytes=VMEM_BUDGET // 4),
    )(mask, act, act_other, weights, *halves)
    cot_late, mixed0 = lax.optimization_barrier((cot_late, mixed0))
    cot = jnp.concatenate((held[1], cot_late))
    cot_other = lax.ppermute(cot, "col", [(0, 1), (1, 0)])
    incoming = pl.pallas_call(
        functools.partial(incoming_kernel, n, rows, cols, blocks),
        out_shape=[pairs_of] * 7,
        in_specs=[vmem] * 5,
        out_specs=[vmem] * 7,
        compiler_params=pltpu.CompilerParams(vmem_limit_bytes=VMEM_BUDGET // 4),
    )(mask, weights, act_full, gate0, mixed0)
    kept = (left, right, gate0, mixed0, *incoming)
    return pl.pallas_call(
        functools.partial(backward_kernel, n, rows, cols, blocks),
        out_shape=jax.ShapeDtypeStruct(pair_act.shape, BF16),
        in_specs=[vmem] * 16,
        out_specs=vmem,
        scratch_shapes=[full] * 3 + [some, some, twice, twice, twice],
        compiler_params=pltpu.CompilerParams(vmem_limit_bytes=VMEM_BUDGET // 2),
    )(mask, act, cot, cot_other, weights, *kept)


def body(pair_act, cotangent, residue_mask, front_weight, out_weight):
    n = residue_mask.shape[0]
    row_count = lax.axis_size("row")
    fits = 20 * n * (n + PAD) * H * 4 <= VMEM_BUDGET
    doubling = row_count >= 4 and row_count & (row_count - 1) == 0 and lax.axis_size("col") == 2
    run = whole_body if fits and doubling else spread_body
    return run(pair_act, cotangent, residue_mask, front_weight, out_weight)


def solution(mesh):
    placed = (P(("grp", "row"), "col", None), P(("grp", "row"), "col", None), P("grp"), P(), P())
    return jax.shard_map(
        body, mesh=mesh, in_specs=placed, out_specs=P(("grp", "row"), "col", None), check_vma=False
    )
```

profile of v0, /device:TPU:0, one launch (start us, length us, event | category | flops | bytes accessed | tf_op | source)
XLA Modules:
  0.0 27.0 jit_solution(7244108932864211898)
XLA Ops:
  0.0 3.1 %collective-permute-start = (bf16[1,4,16,128]{3,2,1,0:T(8,128)(2,1)}, bf16[1,4,16,128]{3,2,1,0:T(8,128)(2,1)S(1)}, u32[]{:S(2)}, u32[]{:S(2)}) collective-permute-start(bf16[1,4,16,128]{3,2,1,0:T(8,128)(2,1)} %bitcast.10), channel_id=1, source_target_pairs={{0,4},{2,6},{4,0},{6,2},{8,12},{10,14},{12,8},{14,10},{1,5},{3,7},... | collective-permute-start | bytes 49160 | tf_op jit(solution)/shard_map/ppermute | solution.py:404
  3.1 0.0 collective-permute-start.3
  3.1 0.8 %pad_maximum_fusion.4 = bf16[2,1,4,16,128]{4,3,2,1,0:T(8,128)(2,1)S(1)} fusion(bf16[1,1,4,16,128]{4,3,2,1,0:T(8,128)(2,1)} %bitcast.13, bf16[1,1,4,16,128]{4,3,2,1,0:T(8,128)(2,1)} %bitcast.11), kind=kLoop, calls=%fused_computation.4 | loop fusion | flops 16384 | bytes 65536 | tf_op jit(solution)/shard_map/stack | solution.py:407
  3.8 0.0 copy-start.1
  3.9 0.6 %copy-done.1 = s32[32]{0:T(128)S(1)} copy-done((s32[32]{0:T(128)S(1)}, s32[32]{0:T(128)}, u32[]{:S(2)}) %copy-start.1) | copy-done | bytes 152
  4.5 0.5 %collective-permute-done = bf16[1,4,16,128]{3,2,1,0:T(8,128)(2,1)S(1)} collective-permute-done((bf16[1,4,16,128]{3,2,1,0:T(8,128)(2,1)}, bf16[1,4,16,128]{3,2,1,0:T(8,128)(2,1)S(1)}, u32[]{:S(2)}, u32[]{:S(2)}) %collective-permute-start) | collective-permute-done | bytes 16416 | tf_op jit(solution)/shard_map/ppermute | solution.py:404
  5.0 3.0 %collective-permute-start.1 = (bf16[2,4,16,128]{3,2,1,0:T(8,128)(2,1)S(1)}, bf16[2,4,16,128]{3,2,1,0:T(8,128)(2,1)S(1)}, u32[]{:S(2)}, u32[]{:S(2)}) collective-permute-start(bf16[2,4,16,128]{3,2,1,0:T(8,128)(2,1)S(1)} %pad_maximum_fusion.5), channel_id=1, source_target_pairs={{0,8},{2,10},{4,12},{6,14},{8,0},{10,2},{12,4},{14,6},{1,9},{3,11}... | collective-permute-start | bytes 98312 | tf_op jit(solution)/shard_map/ppermute | solution.py:404
  8.0 1.0 %constant_dynamic-update-slice_fusion.1 = bf16[2,128,768]{2,1,0:T(8,128)(2,1)S(1)} fusion(bf16[2,128,640]{2,1,0:T(8,128)(2,1)} %param.8), kind=kLoop, calls=%fused_computation.10 | loop fusion | bytes 655360
  9.0 0.9 %collective-permute-done.1 = bf16[2,4,16,128]{3,2,1,0:T(8,128)(2,1)S(1)} collective-permute-done((bf16[2,4,16,128]{3,2,1,0:T(8,128)(2,1)S(1)}, bf16[2,4,16,128]{3,2,1,0:T(8,128)(2,1)S(1)}, u32[]{:S(2)}, u32[]{:S(2)}) %collective-permute-start.1) | collective-permute-done | bytes 32800 | tf_op jit(solution)/shard_map/ppermute | solution.py:404
  9.9 1.9 %collective-permute-start.2 = (bf16[4,4,16,128]{3,2,1,0:T(8,128)(2,1)S(1)}, bf16[4,4,16,128]{3,2,1,0:T(8,128)(2,1)S(1)}, u32[]{:S(2)}, u32[]{:S(2)}) collective-permute-start(bf16[4,4,16,128]{3,2,1,0:T(8,128)(2,1)S(1)} %pad_maximum_fusion.2), channel_id=1, source_target_pairs={{0,2},{2,0},{4,6},{6,4},{8,10},{10,8},{12,14},{14,12},{1,3},{3,1},... | collective-permute-start | bytes 196616 | tf_op jit(solution)/shard_map/ppermute | solution.py:404
  11.9 0.0 collective-permute-done.3
  11.9 2.7 %collective-permute-start.4 = (bf16[2,4,16,128]{3,2,1,0:T(8,128)(2,1)S(1)}, bf16[2,4,16,128]{3,2,1,0:T(8,128)(2,1)S(1)}, u32[]{:S(2)}, u32[]{:S(2)}) collective-permute-start(bf16[2,4,16,128]{3,2,1,0:T(8,128)(2,1)S(1)} %pad_maximum_fusion.6), channel_id=1, source_target_pairs={{0,8},{2,10},{4,12},{6,14},{8,0},{10,2},{12,4},{14,6},{1,9},{3,11}... | collective-permute-start | bytes 98312 | tf_op jit(solution)/shard_map/ppermute | solution.py:404
  14.5 0.0 collective-permute-done.2
  14.6 0.0 copy-start
  14.6 0.1 collective-permute-start.6
  14.7 2.1 %collective-permute-done.4 = bf16[2,4,16,128]{3,2,1,0:T(8,128)(2,1)S(1)} collective-permute-done((bf16[2,4,16,128]{3,2,1,0:T(8,128)(2,1)S(1)}, bf16[2,4,16,128]{3,2,1,0:T(8,128)(2,1)S(1)}, u32[]{:S(2)}, u32[]{:S(2)}) %collective-permute-start.4) | collective-permute-done | bytes 32800 | tf_op jit(solution)/shard_map/ppermute | solution.py:404
  16.8 0.3 collective-permute-start.5
  17.0 0.0 copy-done
  17.0 1.3 %shard_map.55 = (f32[512,128]{1,0:T(8,128)S(1)}, f32[512,128]{1,0:T(8,128)S(1)}, f32[512,128]{1,0:T(8,128)S(1)}, f32[1024,128]{1,0:T(8,128)S(1)}) custom-call(f32[1,32]{1,0:T(1,128)S(1)} %convert_bitcast_fusion.mask_ref, bf16[8,4,16,128]{3,2,1,0:T(8,128)(2,1)S(1)} %pad_maximum_fusion.own_ref.act_ref, ...), custom_call_target="tpu_custom_call" | custom-call | tf_op jit(solution)/shard_map/pallas_call | solution.py:423
  18.3 0.0 collective-permute-done.6.other_ref
  18.3 1.3 %shard_map.56 = (f32[1152,128]{1,0:T(8,128)S(1)}, f32[1152,128]{1,0:T(8,128)S(1)}, f32[1152,128]{1,0:T(8,128)S(1)}, f32[1152,128]{1,0:T(8,128)S(1)}, f32[1152,128]{1,0:T(8,128)S(1)}) custom-call(f32[1,32]{1,0:T(1,128)S(1)} %convert_bitcast_fusion.mask_ref, bf16[8,4,16,128]{3,2,1,0:T(8,128)(2,1)S(1)} %pad_maximum_fusion.own_ref.act_ref, ...), custom_call_target="tpu_custom_call" | custom-call | tf_op jit(solution)/shard_map/pallas_call | solution.py:432
  19.7 1.4 %collective-permute-done.5 = bf16[4,4,16,128]{3,2,1,0:T(8,128)(2,1)S(1)} collective-permute-done((bf16[4,4,16,128]{3,2,1,0:T(8,128)(2,1)S(1)}, bf16[4,4,16,128]{3,2,1,0:T(8,128)(2,1)S(1)}, u32[]{:S(2)}, u32[]{:S(2)}) %collective-permute-start.5) | collective-permute-done | bytes 65568 | tf_op jit(solution)/shard_map/ppermute | solution.py:404
  21.1 0.1 collective-permute-start.7
  21.2 2.6 %shard_map.57 = (f32[1152,128]{1,0:T(8,128)S(1)}, f32[1152,128]{1,0:T(8,128)S(1)}, f32[1152,128]{1,0:T(8,128)S(1)}, f32[1152,128]{1,0:T(8,128)S(1)}, f32[1152,12...) custom-call(f32[1,32]{1,0:T(1,128)S(1)} %convert_bitcast_fusion.mask_ref, ...), custom_call_target="tpu_custom_call" | custom-call | tf_op jit(solution)/shard_map/pallas_call | solution.py:443
  23.8 0.0 collective-permute-done.7.other_ref
  23.8 3.1 %shard_map.58 = bf16[4,16,128]{2,1,0:T(8,128)(2,1)} custom-call(f32[1,32]{1,0:T(1,128)S(1)} %convert_bitcast_fusion.mask_ref, bf16[8,4,16,128]{3,2,1,0:T(8,128)(2,1)S(1)} %pad_maximum_fusion.own_ref.act_ref, bf16[8,4,16,128]{3,2,1,0:T(8,128)(2,1)S(1)} %pad_maximum_fusion.1.own_ref, bf16[8,4,16,128]{3,2,1,0:T(8,128)(2,1)S(1)} %collective-permute-done.7.other_ref, ...), custom_call_target="tpu_custom_call" | custom-call | tf_op jit(solution)/shard_map/pallas_call | solution.py:451
  (9 shorter events, 0.1 us)
Async XLA Ops:
  0.0 5.0 %collective-permute-start = (bf16[1,4,16,128]{3,2,1,0:T(8,128)(2,1)}, bf16[1,4,16,128]{3,2,1,0:T(8,128)(2,1)S(1)}, u32[]{:S(2)}, u32[]{:S(2)}) collective-permute-start(bf16[1,4,16,128]{3,2,1,0:T(8,128)(2,1)} %bitcast.10), channel_id=1, source_target_pairs={{0,4},{2,6},{4,0},{6,2},{8,12},{10,14},{12,8},{14,10},{1,5},{3,7},... | collective-permute-start | bytes 49160 | tf_op jit(solution)/shard_map/ppermute | solution.py:404
  3.1 8.8 %collective-permute-start.3 = (bf16[1,4,16,128]{3,2,1,0:T(8,128)(2,1)}, bf16[1,4,16,128]{3,2,1,0:T(8,128)(2,1)S(1)}, u32[]{:S(2)}, u32[]{:S(2)}) collective-permute-start(bf16[1,4,16,128]{3,2,1,0:T(8,128)(2,1)} %bitcast.12), channel_id=1, source_target_pairs={{0,4},{2,6},{4,0},{6,2},{8,12},{10,14},{12,8},{14,10},{1,5},{3,7},... | collective-permute-start | bytes 49160 | tf_op jit(solution)/shard_map/ppermute | solution.py:404
  3.8 0.7 %copy-start.1 = (s32[32]{0:T(128)S(1)}, s32[32]{0:T(128)}, u32[]{:S(2)}) copy-start(s32[32]{0:T(128)} %param.7) | copy-start | bytes 388
  5.0 4.9 %collective-permute-start.1 = (bf16[2,4,16,128]{3,2,1,0:T(8,128)(2,1)S(1)}, bf16[2,4,16,128]{3,2,1,0:T(8,128)(2,1)S(1)}, u32[]{:S(2)}, u32[]{:S(2)}) collective-permute-start(bf16[2,4,16,128]{3,2,1,0:T(8,128)(2,1)S(1)} %pad_maximum_fusion.5), channel_id=1, source_target_pairs={{0,8},{2,10},{4,12},{6,14},{8,0},{10,2},{12,4},{14,6},{1,9},{3,11}... | collective-permute-start | bytes 98312 | tf_op jit(solution)/shard_map/ppermute | solution.py:404
  9.9 4.6 %collective-permute-start.2 = (bf16[4,4,16,128]{3,2,1,0:T(8,128)(2,1)S(1)}, bf16[4,4,16,128]{3,2,1,0:T(8,128)(2,1)S(1)}, u32[]{:S(2)}, u32[]{:S(2)}) collective-permute-start(bf16[4,4,16,128]{3,2,1,0:T(8,128)(2,1)S(1)} %pad_maximum_fusion.2), channel_id=1, source_target_pairs={{0,2},{2,0},{4,6},{6,4},{8,10},{10,8},{12,14},{14,12},{1,3},{3,1},... | collective-permute-start | bytes 196616 | tf_op jit(solution)/shard_map/ppermute | solution.py:404
  11.9 4.9 %collective-permute-start.4 = (bf16[2,4,16,128]{3,2,1,0:T(8,128)(2,1)S(1)}, bf16[2,4,16,128]{3,2,1,0:T(8,128)(2,1)S(1)}, u32[]{:S(2)}, u32[]{:S(2)}) collective-permute-start(bf16[2,4,16,128]{3,2,1,0:T(8,128)(2,1)S(1)} %pad_maximum_fusion.6), channel_id=1, source_target_pairs={{0,8},{2,10},{4,12},{6,14},{8,0},{10,2},{12,4},{14,6},{1,9},{3,11}... | collective-permute-start | bytes 98312 | tf_op jit(solution)/shard_map/ppermute | solution.py:404
  14.6 2.5 %copy-start = (bf16[2,128,128]{2,1,0:T(8,128)(2,1)S(1)}, bf16[2,128,128]{2,1,0:T(8,128)(2,1)}, u32[]{:S(2)}) copy-start(bf16[2,128,128]{2,1,0:T(8,128)(2,1)} %param.9) | copy-start | bytes 196612
  14.6 3.7 %collective-permute-start.6 = (bf16[8,4,16,128]{3,2,1,0:T(8,128)(2,1)S(1)}, bf16[8,4,16,128]{3,2,1,0:T(8,128)(2,1)S(1)}, u32[]{:S(2)}, u32[]{:S(2)}) collective-permute-start(bf16[8,4,16,128]{3,2,1,0:T(8,128)(2,1)S(1)} %pad_maximum_fusion.own_ref.act_ref), channel_id=1, source_target_pairs={{0,1},{1,0},{2,3},{3,2},{4,5},{5,4},{6,7},{7,6},{8,9},{9,8},{10,11... | collective-permute-start | bytes 393224 | tf_op jit(solution)/shard_map/ppermute | solution.py:417
  16.8 4.3 %collective-permute-start.5 = (bf16[4,4,16,128]{3,2,1,0:T(8,128)(2,1)S(1)}, bf16[4,4,16,128]{3,2,1,0:T(8,128)(2,1)S(1)}, u32[]{:S(2)}, u32[]{:S(2)}) collective-permute-start(bf16[4,4,16,128]{3,2,1,0:T(8,128)(2,1)S(1)} %pad_maximum_fusion.3), channel_id=1, source_target_pairs={{0,2},{2,0},{4,6},{6,4},{8,10},{10,8},{12,14},{14,12},{1,3},{3,1},... | collective-permute-start | bytes 196616 | tf_op jit(solution)/shard_map/ppermute | solution.py:404
  21.1 2.7 %collective-permute-start.7 = (bf16[8,4,16,128]{3,2,1,0:T(8,128)(2,1)S(1)}, bf16[8,4,16,128]{3,2,1,0:T(8,128)(2,1)S(1)}, u32[]{:S(2)}, u32[]{:S(2)}) collective-permute-start(bf16[8,4,16,128]{3,2,1,0:T(8,128)(2,1)S(1)} %pad_maximum_fusion.1.own_ref), channel_id=1, source_target_pairs={{0,1},{1,0},{2,3},{3,2},{4,5},{5,4},{6,7},{7,6},{8,9},{9,8},{10,11... | collective-permute-start | bytes 393224 | tf_op jit(solution)/shard_map/ppermute | solution.py:442
where the time goes:
time: 27.3 us; the launch traced here: 27 us
  starting transfers between devices  11.1 us (41%)
  Pallas kernels  8.33 us (31%)
  waiting for transfers between devices  4.9 us (18%)
  local copies, waits for them, and re-layouts  1.68 us (6%)
  other arithmetic  0.83 us (3%)
    ppermute x6, starting transfers between devices, swap(): return lax.ppermute(array, 'row', [(i, i ^ step) for i in range(row_count)])  11 us
    ppermute x6, waiting for transfers between devices, swap(): return lax.ppermute(array, 'row', [(i, i ^ step) for i in range(row_count)])  4.89 us
    pallas_call x1, Pallas kernels, whole_body(): pl.pallas_call(functools.partial(backward_kernel, n, rows, cols, blocks),...  3.15 us
    pallas_call x1, Pallas kernels, whole_body(): pl.pallas_call(functools.partial(incoming_kernel, n, rows, cols, blocks),...  2.6 us
    unnamed x5, local copies, waits for them, and re-layouts  1.66 us
    pallas_call x1, Pallas kernels, whole_body(): pl.pallas_call(functools.partial(outgoing_kernel, n, rows, cols, blocks),...  1.33 us
    pallas_call x1, Pallas kernels, whole_body(): pl.pallas_call(functools.partial(half_kernel, n, rows, cols, blocks), out...  1.25 us
    another operation x1, other arithmetic, whole_body(): held = lax.optimization_barrier(jnp.stack(sent))  0.77 us
  transfers between devices with their start and end apart: 8, of which 4 were waited for; matrix products, arithmetic and copies ran while one was open for 7% of the time, Pallas kernels for 19%

commit v1 on v0

--- a/solution.py
+++ b/solution.py
@@ -200,8 +200,8 @@
     normed, _ = normalize(source)
     gate_l, val_l, gate_r, val_r, gate = split(matmul(normed, weight))
     return (
-        rounded(mask * (sigmoid(gate_l) * val_l)),
-        rounded(mask * (sigmoid(gate_r) * val_r)),
+        mask * (sigmoid(gate_l) * val_l),
+        mask * (sigmoid(gate_r) * val_r),
         sigmoid(gate),
     )
 
@@ -322,7 +322,7 @@
         n, rows, cols, blocks, mask_ref)
     front_ref, out_ref = weight_ref.at[:, :, : 5 * H], weight_ref.at[:, :, 5 * H :]
     normed, _ = normalize(get(mixed0))
-    value = rounded(get(act) + get(gate0) * matmul(normed, out_ref[0]))
+    value = get(act) + get(gate0) * matmul(normed, out_ref[0])
     put(mid, 0, value)
     a, b, g = projection(front_ref[1], value, mask_of(n, n, 0, 0))
     put(left1, 0, a)
@@ -398,7 +398,7 @@
     weights = jnp.concatenate((front_weight, out_weight), axis=2)
     mask = residue_mask.reshape(1, n).astype(F32)
     blocks = [0]
-    steps = [1 << b for b in range(1, bits)] + [1]
+    steps = [1] + [1 << b for b in range(bits - 1, 0, -1)]
 
     def swap(array, step):
         return lax.ppermute(array, "row", [(i, i ^ step) for i in range(row_count)])

time: 27.3 us -> 27.7 us (1.015)
  starting transfers between devices: 11.1 us -> 11.8 us
    ppermute x6, starting transfers between devices: 11 us -> 11.6 us  [swap(): return lax.ppermute(array, 'row', [(i, i ^ step) for i in range(row_count)])]
where the time goes in v1:
time: 27.7 us; the launch traced here: 27.3 us
  starting transfers between devices  11.8 us (43%)
  Pallas kernels  8.23 us (30%)
  waiting for transfers between devices  4.73 us (17%)
  local copies, waits for them, and re-layouts  1.68 us (6%)
  other arithmetic  0.83 us (3%)
    ppermute x6, starting transfers between devices, swap(): return lax.ppermute(array, 'row', [(i, i ^ step) for i in range(row_count)])  11.6 us
    ppermute x6, waiting for transfers between devices, swap(): return lax.ppermute(array, 'row', [(i, i ^ step) for i in range(row_count)])  4.72 us
    pallas_call x1, Pallas kernels, whole_body(): pl.pallas_call(functools.partial(backward_kernel, n, rows, cols, blocks),...  3.15 us
    pallas_call x1, Pallas kernels, whole_body(): pl.pallas_call(functools.partial(incoming_kernel, n, rows, cols, blocks),...  2.51 us
    unnamed x5, local copies, waits for them, and re-layouts  1.66 us
    pallas_call x1, Pallas kernels, whole_body(): pl.pallas_call(functools.partial(outgoing_kernel, n, rows, cols, blocks),...  1.36 us
    pallas_call x1, Pallas kernels, whole_body(): pl.pallas_call(functools.partial(half_kernel, n, rows, cols, blocks), out...  1.22 us
    another operation x1, other arithmetic, whole_body(): held = lax.optimization_barrier(jnp.stack(sent))  0.77 us
  transfers between devices with their start and end apart: 8, of which 4 were waited for; matrix products, arithmetic and copies ran while one was open for 7% of the time, Pallas kernels for 19%

profile of v1, /device:TPU:0, one launch (start us, length us, event | category | flops | bytes accessed | tf_op | source)
XLA Modules:
  0.0 27.3 jit_solution(8926413337383365423)
XLA Ops:
  0.0 3.0 %collective-permute-start = (bf16[1,4,16,128]{3,2,1,0:T(8,128)(2,1)}, bf16[1,4,16,128]{3,2,1,0:T(8,128)(2,1)S(1)}, u32[]{:S(2)}, u32[]{:S(2)}) collective-permute-start(bf16[1,4,16,128]{3,2,1,0:T(8,128)(2,1)} %bitcast.10), channel_id=1, source_target_pairs={{0,2},{2,0},{4,6},{6,4},{8,10},{10,8},{12,14},{14,12},{1,3},{3,1},... | collective-permute-start | bytes 49160 | tf_op jit(solution)/shard_map/ppermute | solution.py:404
  3.0 0.0 collective-permute-start.3
  3.0 0.8 %pad_maximum_fusion.4 = bf16[2,1,4,16,128]{4,3,2,1,0:T(8,128)(2,1)S(1)} fusion(bf16[1,1,4,16,128]{4,3,2,1,0:T(8,128)(2,1)} %bitcast.13, bf16[1,1,4,16,128]{4,3,2,1,0:T(8,128)(2,1)} %bitcast.11), kind=kLoop, calls=%fused_computation.4 | loop fusion | flops 16384 | bytes 65536 | tf_op jit(solution)/shard_map/stack | solution.py:407
  3.8 0.0 copy-start.1
  3.8 0.6 %copy-done.1 = s32[32]{0:T(128)S(1)} copy-done((s32[32]{0:T(128)S(1)}, s32[32]{0:T(128)}, u32[]{:S(2)}) %copy-start.1) | copy-done | bytes 152
  4.4 0.5 %collective-permute-done = bf16[1,4,16,128]{3,2,1,0:T(8,128)(2,1)S(1)} collective-permute-done((bf16[1,4,16,128]{3,2,1,0:T(8,128)(2,1)}, bf16[1,4,16,128]{3,2,1,0:T(8,128)(2,1)S(1)}, u32[]{:S(2)}, u32[]{:S(2)}) %collective-permute-start) | collective-permute-done | bytes 16416 | tf_op jit(solution)/shard_map/ppermute | solution.py:404
  4.9 3.2 %collective-permute-start.1 = (bf16[2,4,16,128]{3,2,1,0:T(8,128)(2,1)S(1)}, bf16[2,4,16,128]{3,2,1,0:T(8,128)(2,1)S(1)}, u32[]{:S(2)}, u32[]{:S(2)}) collective-permute-start(bf16[2,4,16,128]{3,2,1,0:T(8,128)(2,1)S(1)} %pad_maximum_fusion.5), channel_id=1, source_target_pairs={{0,8},{2,10},{4,12},{6,14},{8,0},{10,2},{12,4},{14,6},{1,9},{3,11}... | collective-permute-start | bytes 98312 | tf_op jit(solution)/shard_map/ppermute | solution.py:404
  8.1 1.0 %constant_dynamic-update-slice_fusion.1 = bf16[2,128,768]{2,1,0:T(8,128)(2,1)S(1)} fusion(bf16[2,128,640]{2,1,0:T(8,128)(2,1)} %param.8), kind=kLoop, calls=%fused_computation.10 | loop fusion | bytes 655360
  9.1 0.9 %collective-permute-done.1 = bf16[2,4,16,128]{3,2,1,0:T(8,128)(2,1)S(1)} collective-permute-done((bf16[2,4,16,128]{3,2,1,0:T(8,128)(2,1)S(1)}, bf16[2,4,16,128]{3,2,1,0:T(8,128)(2,1)S(1)}, u32[]{:S(2)}, u32[]{:S(2)}) %collective-permute-start.1) | collective-permute-done | bytes 32800 | tf_op jit(solution)/shard_map/ppermute | solution.py:404
  10.0 2.0 %collective-permute-start.2 = (bf16[4,4,16,128]{3,2,1,0:T(8,128)(2,1)S(1)}, bf16[4,4,16,128]{3,2,1,0:T(8,128)(2,1)S(1)}, u32[]{:S(2)}, u32[]{:S(2)}) collective-permute-start(bf16[4,4,16,128]{3,2,1,0:T(8,128)(2,1)S(1)} %pad_maximum_fusion.2), channel_id=1, source_target_pairs={{0,4},{2,6},{4,0},{6,2},{8,12},{10,14},{12,8},{14,10},{1,5},{3,7},... | collective-permute-start | bytes 196616 | tf_op jit(solution)/shard_map/ppermute | solution.py:404
  12.0 0.0 collective-permute-done.3
  12.0 2.9 %collective-permute-start.4 = (bf16[2,4,16,128]{3,2,1,0:T(8,128)(2,1)S(1)}, bf16[2,4,16,128]{3,2,1,0:T(8,128)(2,1)S(1)}, u32[]{:S(2)}, u32[]{:S(2)}) collective-permute-start(bf16[2,4,16,128]{3,2,1,0:T(8,128)(2,1)S(1)} %pad_maximum_fusion.6), channel_id=1, source_target_pairs={{0,8},{2,10},{4,12},{6,14},{8,0},{10,2},{12,4},{14,6},{1,9},{3,11}... | collective-permute-start | bytes 98312 | tf_op jit(solution)/shard_map/ppermute | solution.py:404
  14.9 0.0 collective-permute-done.2
  14.9 0.0 copy-start
  14.9 0.1 collective-permute-start.6
  15.0 2.2 %collective-permute-done.4 = bf16[2,4,16,128]{3,2,1,0:T(8,128)(2,1)S(1)} collective-permute-done((bf16[2,4,16,128]{3,2,1,0:T(8,128)(2,1)S(1)}, bf16[2,4,16,128]{3,2,1,0:T(8,128)(2,1)S(1)}, u32[]{:S(2)}, u32[]{:S(2)}) %collective-permute-start.4) | collective-permute-done | bytes 32800 | tf_op jit(solution)/shard_map/ppermute | solution.py:404
  17.2 0.6 %collective-permute-start.5 = (bf16[4,4,16,128]{3,2,1,0:T(8,128)(2,1)S(1)}, bf16[4,4,16,128]{3,2,1,0:T(8,128)(2,1)S(1)}, u32[]{:S(2)}, u32[]{:S(2)}) collective-permute-start(bf16[4,4,16,128]{3,2,1,0:T(8,128)(2,1)S(1)} %pad_maximum_fusion.3), channel_id=1, source_target_pairs={{0,4},{2,6},{4,0},{6,2},{8,12},{10,14},{12,8},{14,10},{1,5},{3,7},... | collective-permute-start | bytes 196616 | tf_op jit(solution)/shard_map/ppermute | solution.py:404
  17.8 0.0 copy-done
  17.8 1.2 %shard_map.55 = (f32[512,128]{1,0:T(8,128)S(1)}, f32[512,128]{1,0:T(8,128)S(1)}, f32[512,128]{1,0:T(8,128)S(1)}, f32[1024,128]{1,0:T(8,128)S(1)}) custom-call(f32[1,32]{1,0:T(1,128)S(1)} %convert_bitcast_fusion.mask_ref, bf16[8,4,16,128]{3,2,1,0:T(8,128)(2,1)S(1)} %pad_maximum_fusion.own_ref.act_ref, ...), custom_call_target="tpu_custom_call" | custom-call | tf_op jit(solution)/shard_map/pallas_call | solution.py:423
  19.0 0.0 collective-permute-done.6.other_ref
  19.1 1.4 %shard_map.56 = (f32[1152,128]{1,0:T(8,128)S(1)}, f32[1152,128]{1,0:T(8,128)S(1)}, f32[1152,128]{1,0:T(8,128)S(1)}, f32[1152,128]{1,0:T(8,128)S(1)}, f32[1152,128]{1,0:T(8,128)S(1)}) custom-call(f32[1,32]{1,0:T(1,128)S(1)} %convert_bitcast_fusion.mask_ref, bf16[8,4,16,128]{3,2,1,0:T(8,128)(2,1)S(1)} %pad_maximum_fusion.own_ref.act_ref, ...), custom_call_target="tpu_custom_call" | custom-call | tf_op jit(solution)/shard_map/pallas_call | solution.py:432
  20.4 1.1 %collective-permute-done.5 = bf16[4,4,16,128]{3,2,1,0:T(8,128)(2,1)S(1)} collective-permute-done((bf16[4,4,16,128]{3,2,1,0:T(8,128)(2,1)S(1)}, bf16[4,4,16,128]{3,2,1,0:T(8,128)(2,1)S(1)}, u32[]{:S(2)}, u32[]{:S(2)}) %collective-permute-start.5) | collective-permute-done | bytes 65568 | tf_op jit(solution)/shard_map/ppermute | solution.py:404
  21.6 0.1 collective-permute-start.7
  21.7 2.5 %shard_map.57 = (f32[1152,128]{1,0:T(8,128)S(1)}, f32[1152,128]{1,0:T(8,128)S(1)}, f32[1152,128]{1,0:T(8,128)S(1)}, f32[1152,128]{1,0:T(8,128)S(1)}, f32[1152,12...) custom-call(f32[1,32]{1,0:T(1,128)S(1)} %convert_bitcast_fusion.mask_ref, ...), custom_call_target="tpu_custom_call" | custom-call | tf_op jit(solution)/shard_map/pallas_call | solution.py:443
  24.2 0.0 collective-permute-done.7.other_ref
  24.2 3.1 %shard_map.58 = bf16[4,16,128]{2,1,0:T(8,128)(2,1)} custom-call(f32[1,32]{1,0:T(1,128)S(1)} %convert_bitcast_fusion.mask_ref, bf16[8,4,16,128]{3,2,1,0:T(8,128)(2,1)S(1)} %pad_maximum_fusion.own_ref.act_ref, bf16[8,4,16,128]{3,2,1,0:T(8,128)(2,1)S(1)} %pad_maximum_fusion.1.own_ref, bf16[8,4,16,128]{3,2,1,0:T(8,128)(2,1)S(1)} %collective-permute-done.7.other_ref, ...), custom_call_target="tpu_custom_call" | custom-call | tf_op jit(solution)/shard_map/pallas_call | solution.py:451
  (9 shorter events, 0.1 us)
Async XLA Ops:
  0.0 4.9 %collective-permute-start = (bf16[1,4,16,128]{3,2,1,0:T(8,128)(2,1)}, bf16[1,4,16,128]{3,2,1,0:T(8,128)(2,1)S(1)}, u32[]{:S(2)}, u32[]{:S(2)}) collective-permute-start(bf16[1,4,16,128]{3,2,1,0:T(8,128)(2,1)} %bitcast.10), channel_id=1, source_target_pairs={{0,2},{2,0},{4,6},{6,4},{8,10},{10,8},{12,14},{14,12},{1,3},{3,1},... | collective-permute-start | bytes 49160 | tf_op jit(solution)/shard_map/ppermute | solution.py:404
  3.0 9.0 %collective-permute-start.3 = (bf16[1,4,16,128]{3,2,1,0:T(8,128)(2,1)}, bf16[1,4,16,128]{3,2,1,0:T(8,128)(2,1)S(1)}, u32[]{:S(2)}, u32[]{:S(2)}) collective-permute-start(bf16[1,4,16,128]{3,2,1,0:T(8,128)(2,1)} %bitcast.12), channel_id=1, source_target_pairs={{0,2},{2,0},{4,6},{6,4},{8,10},{10,8},{12,14},{14,12},{1,3},{3,1},... | collective-permute-start | bytes 49160 | tf_op jit(solution)/shard_map/ppermute | solution.py:404
  3.8 0.7 %copy-start.1 = (s32[32]{0:T(128)S(1)}, s32[32]{0:T(128)}, u32[]{:S(2)}) copy-start(s32[32]{0:T(128)} %param.7) | copy-start | bytes 388
  4.9 5.1 %collective-permute-start.1 = (bf16[2,4,16,128]{3,2,1,0:T(8,128)(2,1)S(1)}, bf16[2,4,16,128]{3,2,1,0:T(8,128)(2,1)S(1)}, u32[]{:S(2)}, u32[]{:S(2)}) collective-permute-start(bf16[2,4,16,128]{3,2,1,0:T(8,128)(2,1)S(1)} %pad_maximum_fusion.5), channel_id=1, source_target_pairs={{0,8},{2,10},{4,12},{6,14},{8,0},{10,2},{12,4},{14,6},{1,9},{3,11}... | collective-permute-start | bytes 98312 | tf_op jit(solution)/shard_map/ppermute | solution.py:404
  10.0 4.9 %collective-permute-start.2 = (bf16[4,4,16,128]{3,2,1,0:T(8,128)(2,1)S(1)}, bf16[4,4,16,128]{3,2,1,0:T(8,128)(2,1)S(1)}, u32[]{:S(2)}, u32[]{:S(2)}) collective-permute-start(bf16[4,4,16,128]{3,2,1,0:T(8,128)(2,1)S(1)} %pad_maximum_fusion.2), channel_id=1, source_target_pairs={{0,4},{2,6},{4,0},{6,2},{8,12},{10,14},{12,8},{14,10},{1,5},{3,7},... | collective-permute-start | bytes 196616 | tf_op jit(solution)/shard_map/ppermute | solution.py:404
  12.0 5.2 %collective-permute-start.4 = (bf16[2,4,16,128]{3,2,1,0:T(8,128)(2,1)S(1)}, bf16[2,4,16,128]{3,2,1,0:T(8,128)(2,1)S(1)}, u32[]{:S(2)}, u32[]{:S(2)}) collective-permute-start(bf16[2,4,16,128]{3,2,1,0:T(8,128)(2,1)S(1)} %pad_maximum_fusion.6), channel_id=1, source_target_pairs={{0,8},{2,10},{4,12},{6,14},{8,0},{10,2},{12,4},{14,6},{1,9},{3,11}... | collective-permute-start | bytes 98312 | tf_op jit(solution)/shard_map/ppermute | solution.py:404
  14.9 2.9 %copy-start = (bf16[2,128,128]{2,1,0:T(8,128)(2,1)S(1)}, bf16[2,128,128]{2,1,0:T(8,128)(2,1)}, u32[]{:S(2)}) copy-start(bf16[2,128,128]{2,1,0:T(8,128)(2,1)} %param.9) | copy-start | bytes 196612
  14.9 4.1 %collective-permute-start.6 = (bf16[8,4,16,128]{3,2,1,0:T(8,128)(2,1)S(1)}, bf16[8,4,16,128]{3,2,1,0:T(8,128)(2,1)S(1)}, u32[]{:S(2)}, u32[]{:S(2)}) collective-permute-start(bf16[8,4,16,128]{3,2,1,0:T(8,128)(2,1)S(1)} %pad_maximum_fusion.own_ref.act_ref), channel_id=1, source_target_pairs={{0,1},{1,0},{2,3},{3,2},{4,5},{5,4},{6,7},{7,6},{8,9},{9,8},{10,11... | collective-permute-start | bytes 393224 | tf_op jit(solution)/shard_map/ppermute | solution.py:417
  17.2 4.3 %collective-permute-start.5 = (bf16[4,4,16,128]{3,2,1,0:T(8,128)(2,1)S(1)}, bf16[4,4,16,128]{3,2,1,0:T(8,128)(2,1)S(1)}, u32[]{:S(2)}, u32[]{:S(2)}) collective-permute-start(bf16[4,4,16,128]{3,2,1,0:T(8,128)(2,1)S(1)} %pad_maximum_fusion.3), channel_id=1, source_target_pairs={{0,4},{2,6},{4,0},{6,2},{8,12},{10,14},{12,8},{14,10},{1,5},{3,7},... | collective-permute-start | bytes 196616 | tf_op jit(solution)/shard_map/ppermute | solution.py:404
  21.6 2.6 %collective-permute-start.7 = (bf16[8,4,16,128]{3,2,1,0:T(8,128)(2,1)S(1)}, bf16[8,4,16,128]{3,2,1,0:T(8,128)(2,1)S(1)}, u32[]{:S(2)}, u32[]{:S(2)}) collective-permute-start(bf16[8,4,16,128]{3,2,1,0:T(8,128)(2,1)S(1)} %pad_maximum_fusion.1.own_ref), channel_id=1, source_target_pairs={{0,1},{1,0},{2,3},{3,2},{4,5},{5,4},{6,7},{7,6},{8,9},{9,8},{10,11... | collective-permute-start | bytes 393224 | tf_op jit(solution)/shard_map/ppermute | solution.py:442
